TPU v7x, 32 devices: a whole 2x2x4 slice. The times are simulated.
32 devices in a mesh: band: 4 (over y, core), space: 8 (over z, x).
Axes of the slice: x: 2, y: 2, z: 4, core: 2. Of those that a mesh axis runs over, the one named last changes fastest.
Arguments:
- states: float32 [256, 48, 1024], P('band', 'space'), may hold values from -6 to 6
- patch_ids: int32 [48, 32], P('space'), may hold values from 0 to 63
- metric_table: float32 [64, 96], replicated, may hold values from 0.5 to 2
- potential: float32 [48, 1024], P('space'), may hold values from -3 to 0
Outputs:
- orthonormal: float32 [256, 48, 1024], P(None, 'space', 'band')
All inputs are finite; a program needn't handle non-finite values.
Results may differ from a plain program's by a relative error of at most 0.00014.
Values sent between devices are 32-bit elements; how exact they have to be, the bound alone decides.
A program may use at most 64 MiB of HBM per device.

v0:
```python
import jax
import jax.numpy as jnp
from jax import lax
from jax.sharding import PartitionSpec as P

DEGREE = 3
NY = 32
NZ = 32
CENTRE = 8.5
HALF_WIDTH = 7.5
OFFSETS = (-2, -1, 0, 1, 2)
WEIGHTS = (-1.0 / 12.0, 4.0 / 3.0, -2.5, 4.0 / 3.0, -1.0 / 12.0)


def with_halo(cells, sides, width):
    for axis, dim in sides:
        count = lax.axis_size(axis)
        ends = count - 1
        head = lax.slice_in_dim(cells, 0, width, axis=dim)
        tail = lax.slice_in_dim(cells, cells.shape[dim] - width, cells.shape[dim], axis=dim)
        cells = jnp.concatenate(
            [
                lax.ppermute(tail, axis, [(i, (i + 1) % count) for i in range(ends)]),
                cells,
                lax.ppermute(head, axis, [((i + 1) % count, i) for i in range(ends)]),
            ],
            axis=dim,
        )
    return cells


def swapped(value, axis, bit):
    mask = 2**bit
    pairs = [(source, source ^ mask) for source in range(lax.axis_size(axis))]
    return lax.ppermute(value, axis, pairs)


def apply_ham(extended, potential, metric, z_weights):
    planes = extended.shape[1] - 4
    plane_cells = extended.shape[2]
    block = extended[:, 2 : 2 + planes, :]
    row_pad = 2 * NZ
    padded = jnp.pad(block, ((0, 0), (0, 0), (row_pad, row_pad)))
    x_term = WEIGHTS[0] * extended[:, 2 + OFFSETS[0] : 2 + OFFSETS[0] + planes, :]
    y_term = (
        WEIGHTS[0]
        * padded[:, :, row_pad + OFFSETS[0] * NZ : row_pad + OFFSETS[0] * NZ + plane_cells]
    )
    z_term = z_weights[0] * padded[:, :, row_pad + OFFSETS[0] : row_pad + OFFSETS[0] + plane_cells]
    for position in range(1, 5):
        offset = OFFSETS[position]
        weight = WEIGHTS[position]
        x_term = x_term + weight * extended[:, 2 + offset : 2 + offset + planes, :]
        y_term = (
            y_term
            + weight * padded[:, :, row_pad + offset * NZ : row_pad + offset * NZ + plane_cells]
        )
        z_term = (
            z_term
            + z_weights[position] * padded[:, :, row_pad + offset : row_pad + offset + plane_cells]
        )
    kinetic = metric[0] * x_term + metric[1] * y_term + metric[2] * z_term
    return potential * block - 0.5 * kinetic


def on_device(states, patch_ids, metric_table, potential):
    planes = states.shape[1]
    plane_cells = states.shape[2]
    one_hot = (patch_ids[:, :, None] == jnp.arange(metric_table.shape[0], dtype=jnp.int32)).astype(
        jnp.float32
    )
    looked = jnp.einsum("xyp,pm->xym", one_hot, metric_table, precision=lax.Precision.HIGHEST)
    metric = looked.reshape(planes, NY, 3, NZ).transpose(2, 0, 1, 3).reshape(3, planes, plane_cells)
    z_index = jnp.arange(plane_cells, dtype=jnp.int32) % NZ
    z_weights = [
        WEIGHTS[position]
        * ((z_index + OFFSETS[position] >= 0) & (z_index + OFFSETS[position] < NZ)).astype(
            jnp.float32
        )
        for position in range(5)
    ]

    def step_ham(block):
        extended = with_halo(block, (("space", 1),), 2)
        return apply_ham(extended, potential, metric, z_weights)

    applied = step_ham(states)
    earlier = states
    current = (applied - CENTRE * states) / HALF_WIDTH
    for degree_step in range(DEGREE - 1):
        applied = step_ham(current)
        following = 2.0 * (applied - CENTRE * current) / HALF_WIDTH - earlier
        earlier = current
        current = following
    regrouped = lax.all_to_all(current, "band", split_axis=2, concat_axis=0, tiled=True)
    all_states = regrouped.shape[0]
    flat = regrouped.reshape(all_states, -1)
    cell_total = planes * plane_cells * lax.axis_size("space")
    local_gram = jnp.dot(
        flat, flat.T, precision=lax.Precision.HIGHEST, preferred_element_type=jnp.float32
    )
    device_index = lax.axis_index(("band", "space"))
    levels = lax.axis_size(("band", "space")).bit_length() - 1
    vector = local_gram.reshape(-1)
    for level in range(levels):
        bit = levels - 1 - level
        half = vector.shape[0] // 2
        upper_side = device_index >> bit & 1 == 1
        kept = jnp.where(upper_side, vector[half:], vector[:half])
        sending = jnp.where(upper_side, vector[:half], vector[half:])
        vector = kept + swapped(sending, ("band", "space"), bit)
    for level in range(levels):
        bit = level
        upper_side = device_index >> bit & 1 == 1
        received = swapped(vector, ("band", "space"), bit)
        vector = jnp.where(
            upper_side, jnp.concatenate([received, vector]), jnp.concatenate([vector, received])
        )
    gram = vector.reshape(all_states, all_states) / cell_total
    factor = jnp.linalg.cholesky(gram)
    result = lax.linalg.triangular_solve(factor, flat, left_side=True, lower=True)
    return result.reshape(all_states, planes, regrouped.shape[2])


def solution(mesh):
    return jax.shard_map(
        on_device,
        mesh=mesh,
        in_specs=(P("band", "space", None), P("space", None), P(), P("space", None)),
        out_specs=P(None, "space", "band"),
        check_vma=False,
    )
```

profile of v0, /device:TPU:0, one launch (start us, length us, event | category | flops | bytes accessed | tf_op | source)
XLA Modules:
  0.0 248.5 jit_solution(1068636462713036321)
XLA Ops:
  2.3 5.0 %collective-permute-start = (f32[64,2,1024]{2,0,1:T(8,128)}, f32[64,2,1024]{2,0,1:T(8,128)S(1)}, u32[]{:S(2)}, u32[]{:S(2)}) collective-permute-start(f32[64,2,1024]{2,0,1:T(8,128)} %get-tuple-element.36), channel_id=1, source_target_pairs={{0,1},{1,2},{2,3},{3,4},{4,5},{5,6},{6,7},{8,9},{9,10},{10,11},{11... | collective-permute-start | bytes 1572872 | tf_op jit(solution)/shard_map/ppermute | solution.py:23
  10.3 19.7 %collective-permute-done = f32[64,2,1024]{2,0,1:T(8,128)S(1)} collective-permute-done((f32[64,2,1024]{2,0,1:T(8,128)}, f32[64,2,1024]{2,0,1:T(8,128)S(1)}, u32[]{:S(2)}, u32[]{:S(2)}) %collective-permute-start) | collective-permute-done | bytes 524320 | tf_op jit(solution)/shard_map/ppermute | solution.py:23
  30.8 3.6 %broadcast_multiply_fusion = (f32[64,6,1024]{2,0,1:T(8,128)S(1)}, f32[64,6,1024]{2,0,1:T(8,128)S(1)}) fusion(f32[64,6,1024]{2,0,1:T(8,128)S(1)} %copy-done.1, f32[1024]{0:T(1024)S(1)} %get-tuple-element.48, f32[1024]{0:T(1024)S(1)} %get-tuple-element.49, f32[1024]{0:T(1024)S(1)} %fusion.136, f32[1024]{0:T(1024)S(1)} %get-tuple-element.50, ...), kind=kLoop, calls=%fused_computation.145 | loop fusion | flops 14548992 | bytes 11128832 | tf_op jit(solution)/shard_map/div | solution.py:89
  34.5 4.3 %collective-permute-start.2 = (f32[64,2,1024]{2,0,1:T(8,128)S(1)}, f32[64,2,1024]{2,0,1:T(8,128)S(1)}, u32[]{:S(2)}, u32[]{:S(2)}) collective-permute-start(f32[64,2,1024]{2,0,1:T(8,128)S(1)} %get-tuple-element.32), channel_id=1, source_target_pairs={{0,1},{1,2},{2,3},{3,4},{4,5},{5,6},{6,7},{8,9},{9,10},{10,11},{11... | collective-permute-start | bytes 1572872 | tf_op jit(solution)/shard_map/ppermute | solution.py:23
  40.1 20.2 %collective-permute-done.2 = f32[64,2,1024]{2,0,1:T(8,128)S(1)} collective-permute-done((f32[64,2,1024]{2,0,1:T(8,128)S(1)}, f32[64,2,1024]{2,0,1:T(8,128)S(1)}, u32[]{:S(2)}, u32[]{:S(2)}) %collective-permute-start.2) | collective-permute-done | bytes 524320 | tf_op jit(solution)/shard_map/ppermute | solution.py:23
  60.3 3.8 %fusion.35 = f32[64,6,1024]{2,0,1:T(8,128)S(1)} fusion(f32[64,6,1024]{2,0,1:T(8,128)S(1)} %copy-done.1, f32[64,6,1024]{2,0,1:T(8,128)S(1)} %get-tuple-element.24, f32[64,2,1024]{2,0,1:T(8,128)S(1)} %collective-permute-done.3, f32[64,2,1024]{2,0,1:T(8,128)S(1)} %collective-permute-done.2, f32[64,6,1024]{2,0,1:T(8,128)S(1)} %get-tuple-element.25, ...), kind=kLoop, calls=%fused_computation.70 | loop fusion | flops 16515072 | bytes 7458816 | tf_op jit(solution)/shard_map/sub | solution.py:92
  64.3 4.4 %collective-permute-start.4 = (f32[64,2,1024]{2,0,1:T(8,128)S(1)}, f32[64,2,1024]{2,0,1:T(8,128)S(1)}, u32[]{:S(2)}, u32[]{:S(2)}) collective-permute-start(f32[64,2,1024]{2,0,1:T(8,128)S(1)} %get-tuple-element.30), channel_id=1, source_target_pairs={{0,1},{1,2},{2,3},{3,4},{4,5},{5,6},{6,7},{8,9},{9,10},{10,11},{11... | collective-permute-start | bytes 1572872 | tf_op jit(solution)/shard_map/ppermute | solution.py:23
  70.0 19.4 %collective-permute-done.4 = f32[64,2,1024]{2,0,1:T(8,128)S(1)} collective-permute-done((f32[64,2,1024]{2,0,1:T(8,128)S(1)}, f32[64,2,1024]{2,0,1:T(8,128)S(1)}, u32[]{:S(2)}, u32[]{:S(2)}) %collective-permute-start.4) | collective-permute-done | bytes 524320 | tf_op jit(solution)/shard_map/ppermute | solution.py:23
  89.3 3.8 %fusion.60 = f32[64,6,1024]{2,0,1:T(8,128)S(1)} fusion(f32[64,6,1024]{2,0,1:T(8,128)S(1)} %fusion.35, f32[64,2,1024]{2,0,1:T(8,128)S(1)} %collective-permute-done.5, f32[64,2,1024]{2,0,1:T(8,128)S(1)} %collective-permute-done.4, f32[64,6,1024]{2,0,1:T(8,128)S(1)} %get-tuple-element.25, f32[1024]{0:T(1024)S(1)} %get-tuple-element.48, ...), kind=kLoop, calls=%fused_computation.95 | loop fusion | flops 16908288 | bytes 5885952 | tf_op jit(solution)/shard_map/sub | solution.py:92
  95.9 5.1 %reshape.143 = f32[4,1,98304]{2,1,0:T(1,128)} reshape(f32[1024,6,64]{2,1,0:T(8,128)} %bitcast.60) | data formatting | bytes 3145728
  101.0 3.7 %all-to-all-start = ((f32[4,1,98304]{2,1,0:T(1,128)}), f32[4,1,98304]{2,1,0:T(1,128)S(1)}, u32[]{:S(2)}, u32[]{:S(2)}) async-start(f32[4,1,98304]{2,1,0:T(1,128)} %reshape.143), calls=%async_computation | async-start | bytes 3145728 | tf_op jit(solution)/shard_map/all_to_all | solution.py:95
  104.7 19.8 %all-to-all-done = f32[4,1,98304]{2,1,0:T(1,128)S(1)} async-done(((f32[4,1,98304]{2,1,0:T(1,128)}), f32[4,1,98304]{2,1,0:T(1,128)S(1)}, u32[]{:S(2)}, u32[]{:S(2)}) %all-to-all-start) | async-done | bytes 1572896 | tf_op jit(solution)/shard_map/all_to_all | solution.py:95
  125.1 5.2 %reduce.24 = f32[4,98304]{1,0:T(4,128)S(1)} reduce(f32[4,1,98304]{2,1,0:T(1,128)S(1)} %all-to-all-done, f32[]{:T(128)} %broadcast.404), dimensions={1}, to_apply=%all_to_all.11.reduce_sub_computation | reduce | bytes 3145732 | tf_op jit(solution)/shard_map/all_to_all | solution.py:95
  130.3 3.6 %reshape.144 = f32[1024,6,64]{2,1,0:T(8,128)} reshape(f32[4,98304]{1,0:T(4,128)S(1)} %reduce.24) | data formatting | bytes 3145728
  140.0 4.5 %collective-permute-done.6 = f32[32768]{0:T(1024)S(1)} collective-permute-done((f32[32768]{0:T(1024)S(1)}, f32[32768]{0:T(1024)S(1)}, u32[]{:S(2)}, u32[]{:S(2)}) %collective-permute-start.6) | collective-permute-done | bytes 131104 | tf_op jit(solution)/shard_map/ppermute | solution.py:35
  145.8 8.5 %collective-permute-start.8 = (f32[8192]{0:T(1024)S(1)}, f32[8192]{0:T(1024)S(1)}, u32[]{:S(2)}, u32[]{:S(2)}) collective-permute-start(f32[8192]{0:T(1024)S(1)} %slice_select_fusion.1), channel_id=1, source_target_pairs={{0,4},{1,5},{2,6},{3,7},{4,0},{5,1},{6,2},{7,3},{8,12},{9,13},{10,... | collective-permute-start | bytes 98312 | tf_op jit(solution)/shard_map/ppermute | solution.py:35
  160.2 3.6 %collective-permute-done.10 = f32[2048]{0:T(1024)S(1)} collective-permute-done((f32[2048]{0:T(1024)S(1)}, f32[2048]{0:T(1024)S(1)}, u32[]{:S(2)}, u32[]{:S(2)}) %collective-permute-start.10) | collective-permute-done | bytes 8224 | tf_op jit(solution)/shard_map/ppermute | solution.py:35
  163.9 3.6 %collective-permute-done.11 = f32[2048]{0:T(1024)S(1)} collective-permute-done((f32[2048]{0:T(1024)S(1)}, f32[2048]{0:T(1024)S(1)}, u32[]{:S(2)}, u32[]{:S(2)}) %collective-permute-start.11) | collective-permute-done | bytes 8224 | tf_op jit(solution)/shard_map/ppermute | solution.py:35
  178.4 4.6 %collective-permute-done.15 = f32[32768]{0:T(1024)S(1)} collective-permute-done((f32[32768]{0:T(1024)S(1)}, f32[32768]{0:T(1024)S(1)}, u32[]{:S(2)}, u32[]{:S(2)}) %collective-permute-start.15) | collective-permute-done | bytes 131104 | tf_op jit(solution)/shard_map/ppermute | solution.py:35
  183.4 11.7 %cholesky.50 = f32[128,128]{1,0:T(8,128)S(1)} custom-call(f32[128,128]{1,0:T(8,128)S(1)} %cholesky.118), custom_call_target="Cholesky" | custom-call | tf_op jit(solution)/shard_map/jit(cholesky)/cholesky | solution.py:120
  195.2 9.8 %custom-call.14 = f32[1,128,128]{1,2,0:T(8,128)S(1)} custom-call(f32[1,128,128]{2,1,0:T(8,128)S(1)} %get-tuple-element.43), custom_call_target="InvertDiagBlocksLowerTriangular" | custom-call | tf_op jit(solution)/shard_map/jit(cholesky)/cholesky | solution.py:120
  205.5 12.0 %cholesky.105 = f32[128,128]{1,0:T(8,128)S(1)} custom-call(f32[128,128]{1,0:T(8,128)S(1)} %convolution_subtract_fusion.1), custom_call_target="Cholesky" | custom-call | tf_op jit(solution)/shard_map/jit(cholesky)/cholesky | solution.py:120
  220.2 4.0 %while.1 = (s32[]{:T(128)}, f32[256,256]{1,0:T(8,128)S(1)}, s32[2,2]{1,0:T(2,128)S(1)}, f32[2,128,128]{2,1,0:T(8,128)S(1)}, s32[]{:T(128)}) while((s32[]{:T(128)}, f32[256,256]{1,0:T(8,128)S(1)}, s32[2,2]{1,0:T(2,128)S(1)}, f32[2,128,128]{2,1,0:T(8,128)S(1)}, s32[]{:T(128)}) %tuple.34), condition=%wide.while_cond, body=%wide.while_body.sunk | while | flops 2 | bytes 131181 | solution.py:121
  224.2 19.7 %custom-call.15 = f32[2,128,128]{1,2,0:T(8,128)S(1)} custom-call(f32[2,128,128]{2,1,0:T(8,128)S(1)} %get-tuple-element.12), custom_call_target="InvertDiagBlocksLowerTriangular" | custom-call | tf_op jit(solution)/shard_map/triangular_solve | solution.py:121
  (111 shorter events, 47.0 us)
Async XLA Ops:
  0.0 8.6 %copy-start = (f32[64,96]{1,0:T(8,128)S(1)}, f32[64,96]{1,0:T(8,128)}, u32[]{:S(2)}) copy-start(f32[64,96]{1,0:T(8,128)} %param.6) | copy-start | bytes 73732
  0.0 8.6 %copy-start.3 = (s32[6,32]{1,0:T(8,128)S(1)}, s32[6,32]{1,0:T(8,128)}, u32[]{:S(2)}) copy-start(s32[6,32]{1,0:T(8,128)} %param.5) | copy-start | bytes 2308
  2.3 27.8 %copy-start.1 = (f32[64,6,1024]{2,0,1:T(8,128)S(1)}, f32[64,6,1024]{2,0,1:T(8,128)}, u32[]{:S(2)}) copy-start(f32[64,6,1024]{2,0,1:T(8,128)} %param.4) | copy-start | bytes 4718596
  2.3 27.7 %collective-permute-start = (f32[64,2,1024]{2,0,1:T(8,128)}, f32[64,2,1024]{2,0,1:T(8,128)S(1)}, u32[]{:S(2)}, u32[]{:S(2)}) collective-permute-start(f32[64,2,1024]{2,0,1:T(8,128)} %get-tuple-element.36), channel_id=1, source_target_pairs={{0,1},{1,2},{2,3},{3,4},{4,5},{5,6},{6,7},{8,9},{9,10},{10,11},{11... | collective-permute-start | bytes 1572872 | tf_op jit(solution)/shard_map/ppermute | solution.py:23
  7.3 23.0 %collective-permute-start.1 = (f32[64,2,1024]{2,0,1:T(8,128)}, f32[64,2,1024]{2,0,1:T(8,128)S(1)}, u32[]{:S(2)}, u32[]{:S(2)}) collective-permute-start(f32[64,2,1024]{2,0,1:T(8,128)} %get-tuple-element.37), channel_id=1, source_target_pairs={{1,0},{2,1},{3,2},{4,3},{5,4},{6,5},{7,6},{9,8},{10,9},{11,10},{12... | collective-permute-start | bytes 1572872 | tf_op jit(solution)/shard_map/ppermute | solution.py:25
  30.1 0.8 copy-start.2
  34.5 25.8 %collective-permute-start.2 = (f32[64,2,1024]{2,0,1:T(8,128)S(1)}, f32[64,2,1024]{2,0,1:T(8,128)S(1)}, u32[]{:S(2)}, u32[]{:S(2)}) collective-permute-start(f32[64,2,1024]{2,0,1:T(8,128)S(1)} %get-tuple-element.32), channel_id=1, source_target_pairs={{0,1},{1,2},{2,3},{3,4},{4,5},{5,6},{6,7},{8,9},{9,10},{10,11},{11... | collective-permute-start | bytes 1572872 | tf_op jit(solution)/shard_map/ppermute | solution.py:23
  38.8 21.5 %collective-permute-start.3 = (f32[64,2,1024]{2,0,1:T(8,128)S(1)}, f32[64,2,1024]{2,0,1:T(8,128)S(1)}, u32[]{:S(2)}, u32[]{:S(2)}) collective-permute-start(f32[64,2,1024]{2,0,1:T(8,128)S(1)} %get-tuple-element.33), channel_id=1, source_target_pairs={{1,0},{2,1},{3,2},{4,3},{5,4},{6,5},{7,6},{9,8},{10,9},{11,10},{12... | collective-permute-start | bytes 1572872 | tf_op jit(solution)/shard_map/ppermute | solution.py:25
  64.3 25.1 %collective-permute-start.4 = (f32[64,2,1024]{2,0,1:T(8,128)S(1)}, f32[64,2,1024]{2,0,1:T(8,128)S(1)}, u32[]{:S(2)}, u32[]{:S(2)}) collective-permute-start(f32[64,2,1024]{2,0,1:T(8,128)S(1)} %get-tuple-element.30), channel_id=1, source_target_pairs={{0,1},{1,2},{2,3},{3,4},{4,5},{5,6},{6,7},{8,9},{9,10},{10,11},{11... | collective-permute-start | bytes 1572872 | tf_op jit(solution)/shard_map/ppermute | solution.py:23
  68.7 20.7 %collective-permute-start.5 = (f32[64,2,1024]{2,0,1:T(8,128)S(1)}, f32[64,2,1024]{2,0,1:T(8,128)S(1)}, u32[]{:S(2)}, u32[]{:S(2)}) collective-permute-start(f32[64,2,1024]{2,0,1:T(8,128)S(1)} %get-tuple-element.31), channel_id=1, source_target_pairs={{1,0},{2,1},{3,2},{4,3},{5,4},{6,5},{7,6},{9,8},{10,9},{11,10},{12... | collective-permute-start | bytes 1572872 | tf_op jit(solution)/shard_map/ppermute | solution.py:25
  101.0 23.6 %all-to-all-start = ((f32[4,1,98304]{2,1,0:T(1,128)}), f32[4,1,98304]{2,1,0:T(1,128)S(1)}, u32[]{:S(2)}, u32[]{:S(2)}) async-start(f32[4,1,98304]{2,1,0:T(1,128)} %reshape.143), calls=%async_computation | async-start | bytes 3145728 | tf_op jit(solution)/shard_map/all_to_all | solution.py:95
  139.4 5.0 %collective-permute-start.6 = (f32[32768]{0:T(1024)S(1)}, f32[32768]{0:T(1024)S(1)}, u32[]{:S(2)}, u32[]{:S(2)}) collective-permute-start(f32[32768]{0:T(1024)S(1)} %bitcast.70), channel_id=1, source_target_pairs={{0,16},{1,17},{2,18},{3,19},{4,20},{5,21},{6,22},{7,23},{8,24},{9,... | collective-permute-start | bytes 393224 | tf_op jit(solution)/shard_map/ppermute | solution.py:35
  144.5 1.3 collective-permute-start.7
  145.8 10.4 %collective-permute-start.8 = (f32[8192]{0:T(1024)S(1)}, f32[8192]{0:T(1024)S(1)}, u32[]{:S(2)}, u32[]{:S(2)}) collective-permute-start(f32[8192]{0:T(1024)S(1)} %slice_select_fusion.1), channel_id=1, source_target_pairs={{0,4},{1,5},{2,6},{3,7},{4,0},{5,1},{6,2},{7,3},{8,12},{9,13},{10,... | collective-permute-start | bytes 98312 | tf_op jit(solution)/shard_map/ppermute | solution.py:35
  156.3 3.8 %collective-permute-start.9 = (f32[4096]{0:T(1024)S(1)}, f32[4096]{0:T(1024)S(1)}, u32[]{:S(2)}, u32[]{:S(2)}) collective-permute-start(f32[4096]{0:T(1024)S(1)} %slice_select_fusion.2), channel_id=1, source_target_pairs={{0,2},{1,3},{2,0},{3,1},{4,6},{5,7},{6,4},{7,5},{8,10},{9,11},{10,... | collective-permute-start | bytes 49160 | tf_op jit(solution)/shard_map/ppermute | solution.py:35
  160.1 3.7 %collective-permute-start.10 = (f32[2048]{0:T(1024)S(1)}, f32[2048]{0:T(1024)S(1)}, u32[]{:S(2)}, u32[]{:S(2)}) collective-permute-start(f32[2048]{0:T(1024)S(1)} %slice_select_fusion.3), channel_id=1, source_target_pairs={{0,1},{1,0},{2,3},{3,2},{4,5},{5,4},{6,7},{7,6},{8,9},{9,8},{10,11... | collective-permute-start | bytes 24584 | tf_op jit(solution)/shard_map/ppermute | solution.py:35
  163.8 3.7 %collective-permute-start.11 = (f32[2048]{0:T(1024)S(1)}, f32[2048]{0:T(1024)S(1)}, u32[]{:S(2)}, u32[]{:S(2)}) collective-permute-start(f32[2048]{0:T(1024)S(1)} %select_add_fusion.3), channel_id=1, source_target_pairs={{0,1},{1,0},{2,3},{3,2},{4,5},{5,4},{6,7},{7,6},{8,9},{9,8},{10,11... | collective-permute-start | bytes 24584 | tf_op jit(solution)/shard_map/ppermute | solution.py:35
  167.5 3.7 %collective-permute-start.12 = (f32[4096]{0:T(1024)S(1)}, f32[4096]{0:T(1024)S(1)}, u32[]{:S(2)}, u32[]{:S(2)}) collective-permute-start(f32[4096]{0:T(1024)S(1)} %maximum_select_fusion.6), channel_id=1, source_target_pairs={{0,2},{1,3},{2,0},{3,1},{4,6},{5,7},{6,4},{7,5},{8,10},{9,11},{10,... | collective-permute-start | bytes 49160 | tf_op jit(solution)/shard_map/ppermute | solution.py:35
  171.2 4.8 %collective-permute-start.13 = (f32[8192]{0:T(1024)S(1)}, f32[8192]{0:T(1024)S(1)}, u32[]{:S(2)}, u32[]{:S(2)}) collective-permute-start(f32[8192]{0:T(1024)S(1)} %maximum_select_fusion.5), channel_id=1, source_target_pairs={{0,4},{1,5},{2,6},{3,7},{4,0},{5,1},{6,2},{7,3},{8,12},{9,13},{10,... | collective-permute-start | bytes 98312 | tf_op jit(solution)/shard_map/ppermute | solution.py:35
  176.1 1.3 collective-permute-start.14
  177.4 5.6 %collective-permute-start.15 = (f32[32768]{0:T(1024)S(1)}, f32[32768]{0:T(1024)S(1)}, u32[]{:S(2)}, u32[]{:S(2)}) collective-permute-start(f32[32768]{0:T(1024)S(1)} %maximum_select_fusion.1), channel_id=1, source_target_pairs={{0,16},{1,17},{2,18},{3,19},{4,20},{5,21},{6,22},{7,23},{8,24},{9,... | collective-permute-start | bytes 393224 | tf_op jit(solution)/shard_map/ppermute | solution.py:35
where the time goes:
time: 249 us
  waiting for transfers between devices  104 us (42%)
  other arithmetic  71.6 us (29%)
  starting transfers between devices  38 us (15%)
  local copies, waits for them, and re-layouts  28.1 us (11%)
  matrix products  4.63 us (2%)
    ppermute x3, waiting for transfers between devices, with_halo(): lax.ppermute(tail, axis, [(i, (i + 1) % count) for i in range(ends)])  59.3 us
    another operation x7, other arithmetic, on_device(): factor = jnp.linalg.cholesky(gram)  34.9 us
    ppermute x10, waiting for transfers between devices, swapped(): return lax.ppermute(value, axis, pairs)  25.2 us
    all_to_all x1, waiting for transfers between devices, on_device(): lax.all_to_all(current, 'band', split_axis=2, concat_axis=0, tiled=True)  19.8 us
    another operation x4, other arithmetic, on_device(): lax.linalg.triangular_solve(factor, flat, left_side=True, lower=True)  19.8 us
    ppermute x10, starting transfers between devices, swapped(): return lax.ppermute(value, axis, pairs)  16.7 us
    ppermute x3, starting transfers between devices, with_halo(): lax.ppermute(tail, axis, [(i, (i + 1) % count) for i in range(ends)])  13.8 us
    unnamed x16, local copies, waits for them, and re-layouts  10.5 us
  transfers between devices with their start and end apart: 17, of which 14 were waited for; matrix products, arithmetic and copies ran while one was open for 1% of the time, Pallas kernels for 0%

commit v1 on v0

--- a/solution.py
+++ b/solution.py
@@ -92,7 +92,10 @@
         following = 2.0 * (applied - CENTRE * current) / HALF_WIDTH - earlier
         earlier = current
         current = following
-    regrouped = lax.all_to_all(current, "band", split_axis=2, concat_axis=0, tiled=True)
+    regrouped = jnp.concatenate(
+        lax.all_to_all(jnp.stack(jnp.split(current, lax.axis_size("band"), axis=2)), "band", 0, 0),
+        axis=0,
+    )
     all_states = regrouped.shape[0]
     flat = regrouped.reshape(all_states, -1)
     cell_total = planes * plane_cells * lax.axis_size("space")

time: 249 us -> 231 us (0.928)
  local copies, waits for them, and re-layouts: 28.1 us -> 15.3 us
  other arithmetic: 71.6 us -> 67.7 us
    unnamed x16 -> x14, local copies, waits for them, and re-layouts: 10.5 us -> 1.82 us
    all_to_all x1 -> x0, other arithmetic: 5.21 us -> none  [on_device(): lax.all_to_all(current, 'band', split_axis=2, concat_axis=0, tiled=True)]
    all_to_all x2 -> x1, local copies, waits for them, and re-layouts: 3.82 us -> 0.95 us  [on_device(): lax.all_to_all(jnp.stack(jnp.split(current, lax.axis_size('band'), axis=2...]
    sub x1 -> x0, local copies, waits for them, and re-layouts: 2.72 us -> none  [on_device(): following = 2.0 * (applied - CENTRE * current) / HALF_WIDTH - earlier]
  transfers between devices with their start and end apart: 17 -> 17, of which waited for: 14 -> 14; matrix products, arithmetic and copies ran while one was open for 1% -> 2% of each run, Pallas kernels for 0% -> 0%
where the time goes in v1:
time: 231 us
  waiting for transfers between devices  103 us (45%)
  other arithmetic  67.7 us (29%)
  starting transfers between devices  38.2 us (17%)
  local copies, waits for them, and re-layouts  15.3 us (7%)
  matrix products  4.63 us (2%)
    ppermute x3, waiting for transfers between devices, with_halo(): lax.ppermute(tail, axis, [(i, (i + 1) % count) for i in range(ends)])  59.3 us
    another operation x7, other arithmetic, on_device(): factor = jnp.linalg.cholesky(gram)  34.9 us
    ppermute x10, waiting for transfers between devices, swapped(): return lax.ppermute(value, axis, pairs)  24.1 us
    all_to_all x1, waiting for transfers between devices, on_device(): lax.all_to_all(jnp.stack(jnp.split(current, lax.axis_size('band'), axis=2...  19.8 us
    another operation x4, other arithmetic, on_device(): lax.linalg.triangular_solve(factor, flat, left_side=True, lower=True)  19.8 us
    ppermute x10, starting transfers between devices, swapped(): return lax.ppermute(value, axis, pairs)  16.8 us
    ppermute x3, starting transfers between devices, with_halo(): lax.ppermute(tail, axis, [(i, (i + 1) % count) for i in range(ends)])  13.8 us
    sub x2, other arithmetic, on_device(): following = 2.0 * (applied - CENTRE * current) / HALF_WIDTH - earlier  7.6 us
  transfers between devices with their start and end apart: 17, of which 14 were waited for; matrix products, arithmetic and copies ran while one was open for 2% of the time, Pallas kernels for 0%

profile of v1, /device:TPU:0, one launch (start us, length us, event | category | flops | bytes accessed | tf_op | source)
XLA Modules:
  0.0 231.0 jit_solution(1369829151086823457)
XLA Ops:
  0.0 2.3 fusion.143
  2.3 5.0 %collective-permute-start = (f32[64,2,1024]{2,0,1:T(8,128)}, f32[64,2,1024]{2,0,1:T(8,128)S(1)}, u32[]{:S(2)}, u32[]{:S(2)}) collective-permute-start(f32[64,2,1024]{2,0,1:T(8,128)} %get-tuple-element.40), channel_id=1, source_target_pairs={{0,1},{1,2},{2,3},{3,4},{4,5},{5,6},{6,7},{8,9},{9,10},{10,11},{11... | collective-permute-start | bytes 1572872 | tf_op jit(solution)/shard_map/ppermute | solution.py:23
  10.3 19.7 %collective-permute-done = f32[64,2,1024]{2,0,1:T(8,128)S(1)} collective-permute-done((f32[64,2,1024]{2,0,1:T(8,128)}, f32[64,2,1024]{2,0,1:T(8,128)S(1)}, u32[]{:S(2)}, u32[]{:S(2)}) %collective-permute-start) | collective-permute-done | bytes 524320 | tf_op jit(solution)/shard_map/ppermute | solution.py:23
  30.8 3.6 %broadcast_multiply_fusion = (f32[64,6,1024]{2,0,1:T(8,128)S(1)}, f32[64,6,1024]{2,0,1:T(8,128)S(1)}) fusion(f32[64,6,1024]{2,0,1:T(8,128)S(1)} %copy-done.1, f32[1024]{0:T(1024)S(1)} %get-tuple-element.52, f32[1024]{0:T(1024)S(1)} %get-tuple-element.53, f32[1024]{0:T(1024)S(1)} %fusion.136, f32[1024]{0:T(1024)S(1)} %get-tuple-element.54, ...), kind=kLoop, calls=%fused_computation.146 | loop fusion | flops 14548992 | bytes 11128832 | tf_op jit(solution)/shard_map/div | solution.py:89
  34.5 4.3 %collective-permute-start.2 = (f32[64,2,1024]{2,0,1:T(8,128)S(1)}, f32[64,2,1024]{2,0,1:T(8,128)S(1)}, u32[]{:S(2)}, u32[]{:S(2)}) collective-permute-start(f32[64,2,1024]{2,0,1:T(8,128)S(1)} %get-tuple-element.36), channel_id=1, source_target_pairs={{0,1},{1,2},{2,3},{3,4},{4,5},{5,6},{6,7},{8,9},{9,10},{10,11},{11... | collective-permute-start | bytes 1572872 | tf_op jit(solution)/shard_map/ppermute | solution.py:23
  40.2 20.2 %collective-permute-done.2 = f32[64,2,1024]{2,0,1:T(8,128)S(1)} collective-permute-done((f32[64,2,1024]{2,0,1:T(8,128)S(1)}, f32[64,2,1024]{2,0,1:T(8,128)S(1)}, u32[]{:S(2)}, u32[]{:S(2)}) %collective-permute-start.2) | collective-permute-done | bytes 524320 | tf_op jit(solution)/shard_map/ppermute | solution.py:23
  60.3 3.8 %fusion.35 = f32[64,6,1024]{2,0,1:T(8,128)S(1)} fusion(f32[64,6,1024]{2,0,1:T(8,128)S(1)} %copy-done.1, f32[64,6,1024]{2,0,1:T(8,128)S(1)} %get-tuple-element.24, f32[64,2,1024]{2,0,1:T(8,128)S(1)} %collective-permute-done.3, f32[64,2,1024]{2,0,1:T(8,128)S(1)} %collective-permute-done.2, f32[64,6,1024]{2,0,1:T(8,128)S(1)} %get-tuple-element.25, ...), kind=kLoop, calls=%fused_computation.70 | loop fusion | flops 16515072 | bytes 7458816 | tf_op jit(solution)/shard_map/sub | solution.py:92
  64.3 4.4 %collective-permute-start.4 = (f32[64,2,1024]{2,0,1:T(8,128)S(1)}, f32[64,2,1024]{2,0,1:T(8,128)S(1)}, u32[]{:S(2)}, u32[]{:S(2)}) collective-permute-start(f32[64,2,1024]{2,0,1:T(8,128)S(1)} %get-tuple-element.34), channel_id=1, source_target_pairs={{0,1},{1,2},{2,3},{3,4},{4,5},{5,6},{6,7},{8,9},{9,10},{10,11},{11... | collective-permute-start | bytes 1572872 | tf_op jit(solution)/shard_map/ppermute | solution.py:23
  70.0 19.4 %collective-permute-done.4 = f32[64,2,1024]{2,0,1:T(8,128)S(1)} collective-permute-done((f32[64,2,1024]{2,0,1:T(8,128)S(1)}, f32[64,2,1024]{2,0,1:T(8,128)S(1)}, u32[]{:S(2)}, u32[]{:S(2)}) %collective-permute-start.4) | collective-permute-done | bytes 524320 | tf_op jit(solution)/shard_map/ppermute | solution.py:23
  89.3 3.8 %fusion.60 = f32[64,6,1024]{2,0,1:T(8,128)S(1)} fusion(f32[64,6,1024]{2,0,1:T(8,128)S(1)} %fusion.35, f32[64,2,1024]{2,0,1:T(8,128)S(1)} %collective-permute-done.5, f32[64,2,1024]{2,0,1:T(8,128)S(1)} %collective-permute-done.4, f32[64,6,1024]{2,0,1:T(8,128)S(1)} %get-tuple-element.25, f32[1024]{0:T(1024)S(1)} %get-tuple-element.52, ...), kind=kLoop, calls=%fused_computation.95 | loop fusion | flops 16908288 | bytes 5885952 | tf_op jit(solution)/shard_map/sub | solution.py:92
  94.6 3.7 %all-to-all-start = ((f32[4,64,6,256]{3,1,2,0:T(8,128)}), f32[4,64,6,256]{3,1,2,0:T(8,128)S(1)}, u32[]{:S(2)}, u32[]{:S(2)}) async-start(f32[4,64,6,256]{3,1,2,0:T(8,128)} %pad_maximum_fusion.4), calls=%async_computation | async-start | bytes 3145728 | tf_op jit(solution)/shard_map/all_to_all | solution.py:96
  98.4 19.8 %all-to-all-done = f32[4,64,6,256]{3,1,2,0:T(8,128)S(1)} async-done(((f32[4,64,6,256]{3,1,2,0:T(8,128)}), f32[4,64,6,256]{3,1,2,0:T(8,128)S(1)}, u32[]{:S(2)}, u32[]{:S(2)}) %all-to-all-start) | async-done | bytes 1572896 | tf_op jit(solution)/shard_map/all_to_all | solution.py:96
  121.9 4.5 %collective-permute-done.6 = f32[32768]{0:T(1024)S(1)} collective-permute-done((f32[32768]{0:T(1024)S(1)}, f32[32768]{0:T(1024)S(1)}, u32[]{:S(2)}, u32[]{:S(2)}) %collective-permute-start.6) | collective-permute-done | bytes 131104 | tf_op jit(solution)/shard_map/ppermute | solution.py:35
  127.8 8.5 %collective-permute-start.8 = (f32[8192]{0:T(1024)S(1)}, f32[8192]{0:T(1024)S(1)}, u32[]{:S(2)}, u32[]{:S(2)}) collective-permute-start(f32[8192]{0:T(1024)S(1)} %slice_select_fusion.1), channel_id=1, source_target_pairs={{0,4},{1,5},{2,6},{3,7},{4,0},{5,1},{6,2},{7,3},{8,12},{9,13},{10,... | collective-permute-start | bytes 98312 | tf_op jit(solution)/shard_map/ppermute | solution.py:35
  138.3 2.0 collective-permute-start.9
  142.2 3.6 %collective-permute-done.10 = f32[2048]{0:T(1024)S(1)} collective-permute-done((f32[2048]{0:T(1024)S(1)}, f32[2048]{0:T(1024)S(1)}, u32[]{:S(2)}, u32[]{:S(2)}) %collective-permute-start.10) | collective-permute-done | bytes 8224 | tf_op jit(solution)/shard_map/ppermute | solution.py:35
  145.9 3.6 %collective-permute-done.11 = f32[2048]{0:T(1024)S(1)} collective-permute-done((f32[2048]{0:T(1024)S(1)}, f32[2048]{0:T(1024)S(1)}, u32[]{:S(2)}, u32[]{:S(2)}) %collective-permute-start.11) | collective-permute-done | bytes 8224 | tf_op jit(solution)/shard_map/ppermute | solution.py:35
  153.2 2.9 %collective-permute-start.13 = (f32[8192]{0:T(1024)S(1)}, f32[8192]{0:T(1024)S(1)}, u32[]{:S(2)}, u32[]{:S(2)}) collective-permute-start(f32[8192]{0:T(1024)S(1)} %maximum_select_fusion.5), channel_id=1, source_target_pairs={{0,4},{1,5},{2,6},{3,7},{4,0},{5,1},{6,2},{7,3},{8,12},{9,13},{10,... | collective-permute-start | bytes 98312 | tf_op jit(solution)/shard_map/ppermute | solution.py:35
  160.6 4.4 %collective-permute-done.15 = f32[32768]{0:T(1024)S(1)} collective-permute-done((f32[32768]{0:T(1024)S(1)}, f32[32768]{0:T(1024)S(1)}, u32[]{:S(2)}, u32[]{:S(2)}) %collective-permute-start.15) | collective-permute-done | bytes 131104 | tf_op jit(solution)/shard_map/ppermute | solution.py:35
  165.4 11.7 %cholesky.50 = f32[128,128]{1,0:T(8,128)S(1)} custom-call(f32[128,128]{1,0:T(8,128)S(1)} %cholesky.118), custom_call_target="Cholesky" | custom-call | tf_op jit(solution)/shard_map/jit(cholesky)/cholesky | solution.py:123
  177.1 10.0 %custom-call.14 = f32[1,128,128]{1,2,0:T(8,128)S(1)} custom-call(f32[1,128,128]{2,1,0:T(8,128)S(1)} %get-tuple-element.47), custom_call_target="InvertDiagBlocksLowerTriangular" | custom-call | tf_op jit(solution)/shard_map/jit(cholesky)/cholesky | solution.py:123
  187.6 11.7 %cholesky.105 = f32[128,128]{1,0:T(8,128)S(1)} custom-call(f32[128,128]{1,0:T(8,128)S(1)} %convolution_subtract_fusion.1), custom_call_target="Cholesky" | custom-call | tf_op jit(solution)/shard_map/jit(cholesky)/cholesky | solution.py:123
  202.3 4.3 %while.1 = (s32[]{:T(128)}, f32[256,256]{1,0:T(8,128)S(1)}, s32[2,2]{1,0:T(2,128)S(1)}, f32[2,128,128]{2,1,0:T(8,128)S(1)}, s32[]{:T(128)}) while((s32[]{:T(128)}, f32[256,256]{1,0:T(8,128)S(1)}, s32[2,2]{1,0:T(2,128)S(1)}, f32[2,128,128]{2,1,0:T(8,128)S(1)}, s32[]{:T(128)}) %tuple.37), condition=%wide.while_cond, body=%wide.while_body.sunk | while | flops 2 | bytes 131181 | solution.py:124
  206.6 19.7 %custom-call.15 = f32[2,128,128]{1,2,0:T(8,128)S(1)} custom-call(f32[2,128,128]{2,1,0:T(8,128)S(1)} %get-tuple-element.12), custom_call_target="InvertDiagBlocksLowerTriangular" | custom-call | tf_op jit(solution)/shard_map/triangular_solve | solution.py:124
  (110 shorter events, 36.3 us)
Async XLA Ops:
  0.0 8.6 %copy-start = (f32[64,96]{1,0:T(8,128)S(1)}, f32[64,96]{1,0:T(8,128)}, u32[]{:S(2)}) copy-start(f32[64,96]{1,0:T(8,128)} %param.6) | copy-start | bytes 73732
  0.0 8.6 %copy-start.3 = (s32[6,32]{1,0:T(8,128)S(1)}, s32[6,32]{1,0:T(8,128)}, u32[]{:S(2)}) copy-start(s32[6,32]{1,0:T(8,128)} %param.5) | copy-start | bytes 2308
  2.3 27.8 %copy-start.1 = (f32[64,6,1024]{2,0,1:T(8,128)S(1)}, f32[64,6,1024]{2,0,1:T(8,128)}, u32[]{:S(2)}) copy-start(f32[64,6,1024]{2,0,1:T(8,128)} %param.4) | copy-start | bytes 4718596
  2.3 27.7 %collective-permute-start = (f32[64,2,1024]{2,0,1:T(8,128)}, f32[64,2,1024]{2,0,1:T(8,128)S(1)}, u32[]{:S(2)}, u32[]{:S(2)}) collective-permute-start(f32[64,2,1024]{2,0,1:T(8,128)} %get-tuple-element.40), channel_id=1, source_target_pairs={{0,1},{1,2},{2,3},{3,4},{4,5},{5,6},{6,7},{8,9},{9,10},{10,11},{11... | collective-permute-start | bytes 1572872 | tf_op jit(solution)/shard_map/ppermute | solution.py:23
  7.3 23.0 %collective-permute-start.1 = (f32[64,2,1024]{2,0,1:T(8,128)}, f32[64,2,1024]{2,0,1:T(8,128)S(1)}, u32[]{:S(2)}, u32[]{:S(2)}) collective-permute-start(f32[64,2,1024]{2,0,1:T(8,128)} %get-tuple-element.41), channel_id=1, source_target_pairs={{1,0},{2,1},{3,2},{4,3},{5,4},{6,5},{7,6},{9,8},{10,9},{11,10},{12... | collective-permute-start | bytes 1572872 | tf_op jit(solution)/shard_map/ppermute | solution.py:25
  30.1 0.8 copy-start.2
  34.5 25.8 %collective-permute-start.2 = (f32[64,2,1024]{2,0,1:T(8,128)S(1)}, f32[64,2,1024]{2,0,1:T(8,128)S(1)}, u32[]{:S(2)}, u32[]{:S(2)}) collective-permute-start(f32[64,2,1024]{2,0,1:T(8,128)S(1)} %get-tuple-element.36), channel_id=1, source_target_pairs={{0,1},{1,2},{2,3},{3,4},{4,5},{5,6},{6,7},{8,9},{9,10},{10,11},{11... | collective-permute-start | bytes 1572872 | tf_op jit(solution)/shard_map/ppermute | solution.py:23
  38.8 21.5 %collective-permute-start.3 = (f32[64,2,1024]{2,0,1:T(8,128)S(1)}, f32[64,2,1024]{2,0,1:T(8,128)S(1)}, u32[]{:S(2)}, u32[]{:S(2)}) collective-permute-start(f32[64,2,1024]{2,0,1:T(8,128)S(1)} %get-tuple-element.37), channel_id=1, source_target_pairs={{1,0},{2,1},{3,2},{4,3},{5,4},{6,5},{7,6},{9,8},{10,9},{11,10},{12... | collective-permute-start | bytes 1572872 | tf_op jit(solution)/shard_map/ppermute | solution.py:25
  64.3 25.1 %collective-permute-start.4 = (f32[64,2,1024]{2,0,1:T(8,128)S(1)}, f32[64,2,1024]{2,0,1:T(8,128)S(1)}, u32[]{:S(2)}, u32[]{:S(2)}) collective-permute-start(f32[64,2,1024]{2,0,1:T(8,128)S(1)} %get-tuple-element.34), channel_id=1, source_target_pairs={{0,1},{1,2},{2,3},{3,4},{4,5},{5,6},{6,7},{8,9},{9,10},{10,11},{11... | collective-permute-start | bytes 1572872 | tf_op jit(solution)/shard_map/ppermute | solution.py:23
  68.7 20.7 %collective-permute-start.5 = (f32[64,2,1024]{2,0,1:T(8,128)S(1)}, f32[64,2,1024]{2,0,1:T(8,128)S(1)}, u32[]{:S(2)}, u32[]{:S(2)}) collective-permute-start(f32[64,2,1024]{2,0,1:T(8,128)S(1)} %get-tuple-element.35), channel_id=1, source_target_pairs={{1,0},{2,1},{3,2},{4,3},{5,4},{6,5},{7,6},{9,8},{10,9},{11,10},{12... | collective-permute-start | bytes 1572872 | tf_op jit(solution)/shard_map/ppermute | solution.py:25
  94.6 23.6 %all-to-all-start = ((f32[4,64,6,256]{3,1,2,0:T(8,128)}), f32[4,64,6,256]{3,1,2,0:T(8,128)S(1)}, u32[]{:S(2)}, u32[]{:S(2)}) async-start(f32[4,64,6,256]{3,1,2,0:T(8,128)} %pad_maximum_fusion.4), calls=%async_computation | async-start | bytes 3145728 | tf_op jit(solution)/shard_map/all_to_all | solution.py:96
  121.4 5.0 %collective-permute-start.6 = (f32[32768]{0:T(1024)S(1)}, f32[32768]{0:T(1024)S(1)}, u32[]{:S(2)}, u32[]{:S(2)}) collective-permute-start(f32[32768]{0:T(1024)S(1)} %bitcast.71), channel_id=1, source_target_pairs={{0,16},{1,17},{2,18},{3,19},{4,20},{5,21},{6,22},{7,23},{8,24},{9,... | collective-permute-start | bytes 393224 | tf_op jit(solution)/shard_map/ppermute | solution.py:35
  126.5 1.3 collective-permute-start.7
  127.8 10.4 %collective-permute-start.8 = (f32[8192]{0:T(1024)S(1)}, f32[8192]{0:T(1024)S(1)}, u32[]{:S(2)}, u32[]{:S(2)}) collective-permute-start(f32[8192]{0:T(1024)S(1)} %slice_select_fusion.1), channel_id=1, source_target_pairs={{0,4},{1,5},{2,6},{3,7},{4,0},{5,1},{6,2},{7,3},{8,12},{9,13},{10,... | collective-permute-start | bytes 98312 | tf_op jit(solution)/shard_map/ppermute | solution.py:35
  138.3 3.8 %collective-permute-start.9 = (f32[4096]{0:T(1024)S(1)}, f32[4096]{0:T(1024)S(1)}, u32[]{:S(2)}, u32[]{:S(2)}) collective-permute-start(f32[4096]{0:T(1024)S(1)} %slice_select_fusion.2), channel_id=1, source_target_pairs={{0,2},{1,3},{2,0},{3,1},{4,6},{5,7},{6,4},{7,5},{8,10},{9,11},{10,... | collective-permute-start | bytes 49160 | tf_op jit(solution)/shard_map/ppermute | solution.py:35
  142.1 3.7 %collective-permute-start.10 = (f32[2048]{0:T(1024)S(1)}, f32[2048]{0:T(1024)S(1)}, u32[]{:S(2)}, u32[]{:S(2)}) collective-permute-start(f32[2048]{0:T(1024)S(1)} %slice_select_fusion.3), channel_id=1, source_target_pairs={{0,1},{1,0},{2,3},{3,2},{4,5},{5,4},{6,7},{7,6},{8,9},{9,8},{10,11... | collective-permute-start | bytes 24584 | tf_op jit(solution)/shard_map/ppermute | solution.py:35
  145.8 3.7 %collective-permute-start.11 = (f32[2048]{0:T(1024)S(1)}, f32[2048]{0:T(1024)S(1)}, u32[]{:S(2)}, u32[]{:S(2)}) collective-permute-start(f32[2048]{0:T(1024)S(1)} %select_add_fusion.3), channel_id=1, source_target_pairs={{0,1},{1,0},{2,3},{3,2},{4,5},{5,4},{6,7},{7,6},{8,9},{9,8},{10,11... | collective-permute-start | bytes 24584 | tf_op jit(solution)/shard_map/ppermute | solution.py:35
  149.5 3.7 %collective-permute-start.12 = (f32[4096]{0:T(1024)S(1)}, f32[4096]{0:T(1024)S(1)}, u32[]{:S(2)}, u32[]{:S(2)}) collective-permute-start(f32[4096]{0:T(1024)S(1)} %maximum_select_fusion.6), channel_id=1, source_target_pairs={{0,2},{1,3},{2,0},{3,1},{4,6},{5,7},{6,4},{7,5},{8,10},{9,11},{10,... | collective-permute-start | bytes 49160 | tf_op jit(solution)/shard_map/ppermute | solution.py:35
  153.2 4.8 %collective-permute-start.13 = (f32[8192]{0:T(1024)S(1)}, f32[8192]{0:T(1024)S(1)}, u32[]{:S(2)}, u32[]{:S(2)}) collective-permute-start(f32[8192]{0:T(1024)S(1)} %maximum_select_fusion.5), channel_id=1, source_target_pairs={{0,4},{1,5},{2,6},{3,7},{4,0},{5,1},{6,2},{7,3},{8,12},{9,13},{10,... | collective-permute-start | bytes 98312 | tf_op jit(solution)/shard_map/ppermute | solution.py:35
  158.0 1.3 collective-permute-start.14
  159.4 5.6 %collective-permute-start.15 = (f32[32768]{0:T(1024)S(1)}, f32[32768]{0:T(1024)S(1)}, u32[]{:S(2)}, u32[]{:S(2)}) collective-permute-start(f32[32768]{0:T(1024)S(1)} %maximum_select_fusion.1), channel_id=1, source_target_pairs={{0,16},{1,17},{2,18},{3,19},{4,20},{5,21},{6,22},{7,23},{8,24},{9,... | collective-permute-start | bytes 393224 | tf_op jit(solution)/shard_map/ppermute | solution.py:35
